TPU v7x, 256 devices: a whole 4x4x8 slice. The times are simulated.
256 devices in a mesh: band: 16 (over x_hi, y, core), ga: 16 (over z, x_lo).
Axes of the slice: x: 4 (x_hi: 2, x_lo: 2; x = x_hi * 2 + x_lo), y: 4, z: 8, core: 2. Of those that a mesh axis runs over, the one named last changes fastest.
Arguments:
- coeffs: float32 [1024, 65536], P('band', 'ga'), may hold values from -90 to 90, as said below
Outputs:
- orthonormal: float32 [1024, 65536], P('band', 'ga')
Inputs may be any that keep to these rules, and one draw needn't show every extreme that they name: `coeffs`: bands are linearly independent.
All inputs are finite; a program needn't handle non-finite values.
Results may differ from a plain program's by a relative error of at most 0.00029.
Values sent between devices are 32-bit elements; how exact they have to be, the bound alone decides.
A program may use at most 128 MiB of HBM per device.

v0:
```python
import jax
import jax.numpy as jnp
from jax import lax
from jax.sharding import PartitionSpec as P


def local(coeffs):
    band_rows, width = coeffs.shape
    columns_all = width * lax.axis_size("ga")
    gathered = lax.all_gather(coeffs, "band", axis=0, tiled=True)
    partial_value = (
        jnp.dot(
            coeffs, gathered.T, precision=lax.Precision.HIGHEST, preferred_element_type=jnp.float32
        )
        / columns_all
    )
    summed = lax.psum(partial_value, "ga")
    margin = lax.all_gather(summed, "band", axis=0, tiled=True)
    factor = jnp.linalg.cholesky(margin)
    order = factor.shape[0]
    start = lax.axis_index("band") * band_rows
    row_ids = lax.broadcasted_iota(jnp.int32, (order, band_rows), 0)
    col_ids = lax.broadcasted_iota(jnp.int32, (order, band_rows), 1)
    selector = jnp.where(row_ids == col_ids + start, 1.0, 0.0).astype(jnp.float32)
    solved = lax.linalg.triangular_solve(
        factor, selector, left_side=True, lower=True, transpose_a=True
    )
    own_rows = solved.T
    return jnp.dot(
        own_rows, gathered, precision=lax.Precision.HIGHEST, preferred_element_type=jnp.float32
    )


def solution(mesh):
    return jax.shard_map(
        local, mesh=mesh, in_specs=(P("band", "ga"),), out_specs=P("band", "ga"), check_vma=False
    )
```

profile of v0, /device:TPU:1, one launch (start us, length us, event | category | flops | bytes accessed | tf_op | source)
XLA Modules:
  0.0 702.7 jit_solution(17107480262078073157)
XLA Ops:
  6.5 0.7 all-gather.3.cloned.1.call-update
  7.3 121.3 %all-gather.3.cloned.1.call-done = f32[1024,4096]{1,0:T(8,128)} async-done(((f32[64,4096]{1,0:T(8,128)}), f32[1024,4096]{1,0:T(8,128)}) %all-gather.3.cloned.1.call-update) | async-done | bytes 16777232 | tf_op jit(solution)/shard_map/all_gather | solution.py:10
  128.6 20.5 %convolution_multiply_fusion = f32[64,1024]{1,0:T(8,128)} fusion(f32[64,4096]{1,0:T(8,128)} %param.1, f32[1024,4096]{1,0:T(8,128)} %all-gather.3.cloned.1.call-done), kind=kOutput, calls=%fused_computation.13 | convolution fusion | flops 3221291008 | bytes 18087936 | tf_op jit(solution)/shard_map/dot_general | solution.py:12
  149.2 123.3 %all-reduce.3.cloned.1.call-done = f32[64,1024]{1,0:T(8,128)} async-done(((f32[64,1024]{1,0:T(8,128)}), f32[64,1024]{1,0:T(8,128)}) %all-reduce.3.cloned.1.call-update) | async-done | bytes 262160 | tf_op jit(solution)/shard_map/psum | solution.py:17
  272.6 73.6 %all-gather.5.cloned.1.call-done = f32[1024,1024]{1,0:T(8,128)} async-done(((f32[64,1024]{1,0:T(8,128)}), f32[1024,1024]{1,0:T(8,128)}) %all-gather.5.cloned.1.call-update) | async-done | bytes 4194320 | tf_op jit(solution)/shard_map/all_gather | solution.py:18
  346.3 5.8 copy.4
  352.1 4.4 fusion
  356.5 1.9 copy-done
  358.4 11.7 %cholesky.223 = f32[128,128]{1,0:T(8,128)S(1)} custom-call(f32[128,128]{1,0:T(8,128)S(1)} %cholesky.580), custom_call_target="Cholesky" | custom-call | tf_op jit(solution)/shard_map/jit(cholesky)/cholesky | solution.py:19
  370.2 9.8 %custom-call.62 = f32[1,128,128]{1,2,0:T(8,128)S(1)} custom-call(f32[1,128,128]{2,1,0:T(8,128)S(1)} %get-tuple-element.44), custom_call_target="InvertDiagBlocksLowerTriangular" | custom-call | tf_op jit(solution)/shard_map/jit(cholesky)/cholesky | solution.py:19
  380.0 2.5 cholesky.255
  382.5 2.3 constant_dynamic-update-slice_fusion.32
  384.8 1.5 convolution_subtract_fusion
  386.4 11.9 %cholesky.244 = f32[128,128]{1,0:T(8,128)S(1)} custom-call(f32[128,128]{1,0:T(8,128)S(1)} %cholesky.584), custom_call_target="Cholesky" | custom-call | tf_op jit(solution)/shard_map/jit(cholesky)/cholesky | solution.py:19
  398.9 9.8 %custom-call.63 = f32[1,128,128]{1,2,0:T(8,128)S(1)} custom-call(f32[1,128,128]{2,1,0:T(8,128)S(1)} %get-tuple-element.41), custom_call_target="InvertDiagBlocksLowerTriangular" | custom-call | tf_op jit(solution)/shard_map/jit(cholesky)/cholesky | solution.py:19
  408.7 1.2 convolution_dynamic-update-slice_fusion
  410.0 2.1 convolution_subtract_fusion.1
  412.1 11.7 %cholesky.468 = f32[128,128]{1,0:T(8,128)S(1)} custom-call(f32[128,128]{1,0:T(8,128)S(1)} %cholesky.589), custom_call_target="Cholesky" | custom-call | tf_op jit(solution)/shard_map/jit(cholesky)/cholesky | solution.py:19
  424.4 0.6 compare_reduce_fusion.5
  425.1 9.8 %custom-call.64 = f32[1,128,128]{1,2,0:T(8,128)S(1)} custom-call(f32[1,128,128]{2,1,0:T(8,128)S(1)} %get-tuple-element.38), custom_call_target="InvertDiagBlocksLowerTriangular" | custom-call | tf_op jit(solution)/shard_map/jit(cholesky)/cholesky | solution.py:19
  434.9 1.2 convolution_dynamic-update-slice_fusion.1
  436.1 2.3 convolution_subtract_fusion.2
  438.4 11.9 %cholesky.487 = f32[128,128]{1,0:T(8,128)S(1)} custom-call(f32[128,128]{1,0:T(8,128)S(1)} %cholesky.594), custom_call_target="Cholesky" | custom-call | tf_op jit(solution)/shard_map/jit(cholesky)/cholesky | solution.py:19
  451.6 9.8 %custom-call.65 = f32[1,128,128]{1,2,0:T(8,128)S(1)} custom-call(f32[1,128,128]{2,1,0:T(8,128)S(1)} %get-tuple-element.35), custom_call_target="InvertDiagBlocksLowerTriangular" | custom-call | tf_op jit(solution)/shard_map/jit(cholesky)/cholesky | solution.py:19
  461.4 1.1 convolution_dynamic-update-slice_fusion.2
  462.5 2.4 convolution_subtract_fusion.3
  464.9 11.7 %cholesky.506 = f32[128,128]{1,0:T(8,128)S(1)} custom-call(f32[128,128]{1,0:T(8,128)S(1)} %cholesky.599), custom_call_target="Cholesky" | custom-call | tf_op jit(solution)/shard_map/jit(cholesky)/cholesky | solution.py:19
  476.6 0.7 select_reduce_fusion.3
  477.3 0.7 compare_reduce_fusion.3
  477.9 10.2 %custom-call.66 = f32[1,128,128]{1,2,0:T(8,128)S(1)} custom-call(f32[1,128,128]{2,1,0:T(8,128)S(1)} %get-tuple-element.32), custom_call_target="InvertDiagBlocksLowerTriangular" | custom-call | tf_op jit(solution)/shard_map/jit(cholesky)/cholesky | solution.py:19
  488.1 1.0 convolution_dynamic-update-slice_fusion.3
  489.1 2.3 convolution_subtract_fusion.4
  491.4 11.7 %cholesky.526 = f32[128,128]{1,0:T(8,128)S(1)} custom-call(f32[128,128]{1,0:T(8,128)S(1)} %cholesky.604), custom_call_target="Cholesky" | custom-call | tf_op jit(solution)/shard_map/jit(cholesky)/cholesky | solution.py:19
  504.4 9.8 %custom-call.67 = f32[1,128,128]{1,2,0:T(8,128)S(1)} custom-call(f32[1,128,128]{2,1,0:T(8,128)S(1)} %get-tuple-element.29), custom_call_target="InvertDiagBlocksLowerTriangular" | custom-call | tf_op jit(solution)/shard_map/jit(cholesky)/cholesky | solution.py:19
  514.2 0.9 convolution_dynamic-update-slice_fusion.4
  515.1 2.0 convolution_subtract_fusion.5
  517.2 11.9 %cholesky.546 = f32[128,128]{1,0:T(8,128)S(1)} custom-call(f32[128,128]{1,0:T(8,128)S(1)} %cholesky.609), custom_call_target="Cholesky" | custom-call | tf_op jit(solution)/shard_map/jit(cholesky)/cholesky | solution.py:19
  529.0 0.7 select_reduce_fusion.1
  529.7 0.7 compare_reduce_fusion.1
  530.4 9.8 %custom-call.68 = f32[1,128,128]{1,2,0:T(8,128)S(1)} custom-call(f32[1,128,128]{2,1,0:T(8,128)S(1)} %get-tuple-element.26), custom_call_target="InvertDiagBlocksLowerTriangular" | custom-call | tf_op jit(solution)/shard_map/jit(cholesky)/cholesky | solution.py:19
  540.2 0.8 convolution_dynamic-update-slice_fusion.5
  541.1 1.8 convolution_subtract_fusion.10
  542.8 11.7 %cholesky.564 = f32[128,128]{1,0:T(8,128)S(1)} custom-call(f32[128,128]{1,0:T(8,128)S(1)} %convolution_subtract_fusion.10), custom_call_target="Cholesky" | custom-call | tf_op jit(solution)/shard_map/jit(cholesky)/cholesky | solution.py:19
  554.6 0.6 select_reduce_fusion
  555.8 0.7 compare_reduce_fusion.6
  561.5 4.8 select_select_fusion
  566.3 22.9 %while.1 = (s32[]{:T(128)}, f32[1024,1024]{1,0:T(8,128)}, s32[8,2]{0,1:T(2,128)S(1)}, f32[8,128,128]{2,1,0:T(8,128)S(1)}, s32[]{:T(128)}) while((s32[]{:T(128)}, f32[1024,1024]{1,0:T(8,128)}, s32[8,2]{0,1:T(2,128)S(1)}, f32[8,128,128]{2,1,0:T(8,128)S(1)}, s32[]{:T(128)}) %tuple.38), condition=%wide.while_cond, body=%wide.while_body.sunk | while | flops 2 | bytes 131181 | solution.py:25
  566.9 2.2 bitcast_dynamic-update-slice_fusion.2
  569.8 2.2 bitcast_dynamic-update-slice_fusion.2
  572.6 2.2 bitcast_dynamic-update-slice_fusion.2
  575.5 2.2 bitcast_dynamic-update-slice_fusion.2
  578.4 2.2 bitcast_dynamic-update-slice_fusion.2
  581.3 2.2 bitcast_dynamic-update-slice_fusion.2
  584.1 2.2 bitcast_dynamic-update-slice_fusion.2
  587.0 2.2 bitcast_dynamic-update-slice_fusion.2
  589.2 78.8 %custom-call.69 = f32[8,128,128]{1,2,0:T(8,128)S(1)} custom-call(f32[8,128,128]{2,1,0:T(8,128)S(1)} %get-tuple-element.12), custom_call_target="InvertDiagBlocksLowerTriangular" | custom-call | tf_op jit(solution)/shard_map/triangular_solve | solution.py:25
  668.3 1.1 convolution_subtract_fusion.9
  669.7 1.3 convolution_subtract_fusion.8
  671.3 1.4 convolution_subtract_fusion.7
  673.0 1.5 convolution_subtract_fusion.12
  674.8 1.7 convolution_subtract_fusion.11
  676.8 1.8 convolution_subtract_fusion.13
  679.0 1.9 convolution_subtract_fusion.6
  681.3 14.7 %fusion.63 = f32[64,4096]{1,0:T(8,128)} fusion(f32[1024,64]{0,1:T(8,128)S(1)} %constant_dynamic-update-slice_fusion.18, f32[1024,4096]{1,0:T(8,128)} %all-gather.3.cloned.1.call-done), kind=kOutput, calls=%fused_computation.159 | convolution fusion | flops 3221225472 | bytes 18087936 | tf_op jit(solution)/shard_map/dot_general | solution.py:29
  (72 shorter events, 12.0 us)
Async XLA Ops:
  6.5 122.1 %all-gather.3.cloned.1.call-start = ((), (), s32[]{:S(2)}) async-start(), calls=%async_computation | async-start | bytes 17825792 | tf_op jit(solution)/shard_map/all_gather | solution.py:10
  7.3 265.2 %all-reduce.3.cloned.1.call-start = ((), (), s32[]{:S(2)}) async-start(), calls=%async_computation.1 | async-start | bytes 524288 | tf_op jit(solution)/shard_map/psum | solution.py:17
  149.1 197.2 %all-gather.5.cloned.1.call-start = ((), (), s32[]{:S(2)}) async-start(), calls=%async_computation.2 | async-start | bytes 4456448 | tf_op jit(solution)/shard_map/all_gather | solution.py:18
  356.5 1.9 copy-start
Sparse Core Ops, SparseCore 0:
  10.1 118.4 all-gather.2
  149.2 123.2 all-reduce.2
  275.6 70.5 all-gather.4
where the time goes:
time: 709 us; the launch traced here: 703 us
  waiting for transfers between devices  319 us (45%)
  other arithmetic  260 us (37%)
  matrix products  71.1 us (10%)
  local copies, waits for them, and re-layouts  33.1 us (5%)
  between operations  18.8 us (3%)
    another operation x30, other arithmetic, local(): factor = jnp.linalg.cholesky(margin)  172 us
    psum x1, waiting for transfers between devices, local(): summed = lax.psum(partial_value, 'ga')  123 us
    all_gather x1, waiting for transfers between devices, local(): gathered = lax.all_gather(coeffs, 'band', axis=0, tiled=True)  121 us
    another operation x3, other arithmetic, local(): lax.linalg.triangular_solve(factor, selector, left_side=True, lower=True,...  83.6 us
    all_gather x1, waiting for transfers between devices, local(): margin = lax.all_gather(summed, 'band', axis=0, tiled=True)  73.6 us
    another operation x14, matrix products, local(): factor = jnp.linalg.cholesky(margin)  23.1 us
    another operation x24, local copies, waits for them, and re-layouts  22.7 us
    dot_general x1, matrix products, local(): jnp.dot(coeffs, gathered.T, precision=lax.Precision.HIGHEST, preferred_el...  20.5 us
  transfers between devices with their start and end apart: 3, of which 3 were waited for; matrix products, arithmetic and copies ran while one was open for 0% of the time, Pallas kernels for 0%

commit v1 on v0

--- a/solution.py
+++ b/solution.py
@@ -14,7 +14,7 @@
         )
         / columns_all
     )
-    summed = lax.psum(partial_value, "ga")
+    summed = jnp.sum(lax.all_gather(partial_value, "ga"), axis=0)
     margin = lax.all_gather(summed, "band", axis=0, tiled=True)
     factor = jnp.linalg.cholesky(margin)
     order = factor.shape[0]

time: 709 us -> 673 us (0.949)
  waiting for transfers between devices: 319 us -> 279 us
    psum x1 -> x0, waiting for transfers between devices: 123 us -> none  [local(): summed = lax.psum(partial_value, 'ga')]
    all_gather x0 -> x1, waiting for transfers between devices: none -> 94.6 us  [local(): summed = jnp.sum(lax.all_gather(partial_value, 'ga'), axis=0)]
    all_gather x1, waiting for transfers between devices: 73.6 us -> 62.9 us  [local(): margin = lax.all_gather(summed, 'band', axis=0, tiled=True)]
where the time goes in v1:
time: 673 us; the launch traced here: 666 us
  waiting for transfers between devices  279 us (41%)
  other arithmetic  264 us (39%)
  matrix products  71.1 us (11%)
  local copies, waits for them, and re-layouts  33.3 us (5%)
  between operations  18.7 us (3%)
    another operation x30, other arithmetic, local(): factor = jnp.linalg.cholesky(margin)  172 us
    all_gather x1, waiting for transfers between devices, local(): gathered = lax.all_gather(coeffs, 'band', axis=0, tiled=True)  121 us
    all_gather x1, waiting for transfers between devices, local(): summed = jnp.sum(lax.all_gather(partial_value, 'ga'), axis=0)  94.6 us
    another operation x3, other arithmetic, local(): lax.linalg.triangular_solve(factor, selector, left_side=True, lower=True,...  83.6 us
    all_gather x1, waiting for transfers between devices, local(): margin = lax.all_gather(summed, 'band', axis=0, tiled=True)  62.9 us
    another operation x14, matrix products, local(): factor = jnp.linalg.cholesky(margin)  23.1 us
    another operation x24, local copies, waits for them, and re-layouts  23 us
    dot_general x1, matrix products, local(): jnp.dot(coeffs, gathered.T, precision=lax.Precision.HIGHEST, preferred_el...  20.5 us
  transfers between devices with their start and end apart: 3, of which 3 were waited for; matrix products, arithmetic and copies ran while one was open for 0% of the time, Pallas kernels for 0%

profile of v1, /device:TPU:1, one launch (start us, length us, event | category | flops | bytes accessed | tf_op | source)
XLA Modules:
  0.0 666.5 jit_solution(7737241739669407625)
XLA Ops:
  6.5 0.7 all-gather.5.cloned.1.call-update
  7.3 121.3 %all-gather.5.cloned.1.call-done = f32[1024,4096]{1,0:T(8,128)} async-done(((f32[64,4096]{1,0:T(8,128)}), f32[1024,4096]{1,0:T(8,128)}) %all-gather.5.cloned.1.call-update) | async-done | bytes 16777232 | tf_op jit(solution)/shard_map/all_gather | solution.py:10
  128.6 20.5 %convolution_multiply_fusion = f32[64,1024]{1,0:T(8,128)} fusion(f32[64,4096]{1,0:T(8,128)} %param.1, f32[1024,4096]{1,0:T(8,128)} %all-gather.5.cloned.1.call-done), kind=kOutput, calls=%fused_computation.13 | convolution fusion | flops 3221291008 | bytes 18087936 | tf_op jit(solution)/shard_map/dot_general | solution.py:12
  149.2 94.6 %all-gather.9.cloned.1.call-done = f32[1024,1024]{1,0:T(8,128)} async-done(((f32[64,1024]{1,0:T(8,128)}), f32[1024,1024]{1,0:T(8,128)}) %all-gather.9.cloned.1.call-update) | async-done | bytes 4194320 | tf_op jit(solution)/shard_map/all_gather | solution.py:17
  243.7 3.2 reduce_sum.9
  247.0 62.9 %all-gather.7.cloned.1.call-done = f32[1024,1024]{1,0:T(8,128)} async-done(((f32[64,1024]{1,0:T(8,128)}), f32[1024,1024]{1,0:T(8,128)}) %all-gather.7.cloned.1.call-update) | async-done | bytes 4194320 | tf_op jit(solution)/shard_map/all_gather | solution.py:18
  309.9 5.8 copy.3
  315.7 4.4 fusion
  320.1 1.9 copy-done
  322.0 11.7 %cholesky.223 = f32[128,128]{1,0:T(8,128)S(1)} custom-call(f32[128,128]{1,0:T(8,128)S(1)} %cholesky.580), custom_call_target="Cholesky" | custom-call | tf_op jit(solution)/shard_map/jit(cholesky)/cholesky | solution.py:19
  333.8 2.5 cholesky.255
  336.3 9.8 %custom-call.62 = f32[1,128,128]{1,2,0:T(8,128)S(1)} custom-call(f32[1,128,128]{2,1,0:T(8,128)S(1)} %get-tuple-element.44), custom_call_target="InvertDiagBlocksLowerTriangular" | custom-call | tf_op jit(solution)/shard_map/jit(cholesky)/cholesky | solution.py:19
  346.1 2.4 constant_dynamic-update-slice_fusion.32
  348.5 1.5 convolution_subtract_fusion
  350.0 11.9 %cholesky.244 = f32[128,128]{1,0:T(8,128)S(1)} custom-call(f32[128,128]{1,0:T(8,128)S(1)} %cholesky.584), custom_call_target="Cholesky" | custom-call | tf_op jit(solution)/shard_map/jit(cholesky)/cholesky | solution.py:19
  362.5 9.8 %custom-call.63 = f32[1,128,128]{1,2,0:T(8,128)S(1)} custom-call(f32[1,128,128]{2,1,0:T(8,128)S(1)} %get-tuple-element.41), custom_call_target="InvertDiagBlocksLowerTriangular" | custom-call | tf_op jit(solution)/shard_map/jit(cholesky)/cholesky | solution.py:19
  372.3 1.2 convolution_dynamic-update-slice_fusion
  373.6 2.1 convolution_subtract_fusion.1
  375.7 11.7 %cholesky.468 = f32[128,128]{1,0:T(8,128)S(1)} custom-call(f32[128,128]{1,0:T(8,128)S(1)} %cholesky.589), custom_call_target="Cholesky" | custom-call | tf_op jit(solution)/shard_map/jit(cholesky)/cholesky | solution.py:19
  388.7 9.8 %custom-call.64 = f32[1,128,128]{1,2,0:T(8,128)S(1)} custom-call(f32[1,128,128]{2,1,0:T(8,128)S(1)} %get-tuple-element.38), custom_call_target="InvertDiagBlocksLowerTriangular" | custom-call | tf_op jit(solution)/shard_map/jit(cholesky)/cholesky | solution.py:19
  398.5 1.2 convolution_dynamic-update-slice_fusion.1
  399.7 2.3 convolution_subtract_fusion.2
  402.0 11.9 %cholesky.487 = f32[128,128]{1,0:T(8,128)S(1)} custom-call(f32[128,128]{1,0:T(8,128)S(1)} %cholesky.594), custom_call_target="Cholesky" | custom-call | tf_op jit(solution)/shard_map/jit(cholesky)/cholesky | solution.py:19
  414.6 0.7 compare_reduce_fusion.4
  415.2 9.8 %custom-call.65 = f32[1,128,128]{1,2,0:T(8,128)S(1)} custom-call(f32[1,128,128]{2,1,0:T(8,128)S(1)} %get-tuple-element.35), custom_call_target="InvertDiagBlocksLowerTriangular" | custom-call | tf_op jit(solution)/shard_map/jit(cholesky)/cholesky | solution.py:19
  425.0 1.1 convolution_dynamic-update-slice_fusion.2
  426.1 2.4 convolution_subtract_fusion.3
  428.5 11.7 %cholesky.506 = f32[128,128]{1,0:T(8,128)S(1)} custom-call(f32[128,128]{1,0:T(8,128)S(1)} %cholesky.599), custom_call_target="Cholesky" | custom-call | tf_op jit(solution)/shard_map/jit(cholesky)/cholesky | solution.py:19
  440.2 0.7 select_reduce_fusion.3
  441.5 10.2 %custom-call.66 = f32[1,128,128]{1,2,0:T(8,128)S(1)} custom-call(f32[1,128,128]{2,1,0:T(8,128)S(1)} %get-tuple-element.32), custom_call_target="InvertDiagBlocksLowerTriangular" | custom-call | tf_op jit(solution)/shard_map/jit(cholesky)/cholesky | solution.py:19
  451.7 1.0 convolution_dynamic-update-slice_fusion.3
  452.7 2.3 convolution_subtract_fusion.4
  455.0 11.7 %cholesky.526 = f32[128,128]{1,0:T(8,128)S(1)} custom-call(f32[128,128]{1,0:T(8,128)S(1)} %cholesky.604), custom_call_target="Cholesky" | custom-call | tf_op jit(solution)/shard_map/jit(cholesky)/cholesky | solution.py:19
  467.4 0.7 compare_reduce_fusion.2
  468.1 9.8 %custom-call.67 = f32[1,128,128]{1,2,0:T(8,128)S(1)} custom-call(f32[1,128,128]{2,1,0:T(8,128)S(1)} %get-tuple-element.29), custom_call_target="InvertDiagBlocksLowerTriangular" | custom-call | tf_op jit(solution)/shard_map/jit(cholesky)/cholesky | solution.py:19
  477.9 0.9 convolution_dynamic-update-slice_fusion.4
  478.8 2.0 convolution_subtract_fusion.5
  480.9 11.9 %cholesky.546 = f32[128,128]{1,0:T(8,128)S(1)} custom-call(f32[128,128]{1,0:T(8,128)S(1)} %cholesky.609), custom_call_target="Cholesky" | custom-call | tf_op jit(solution)/shard_map/jit(cholesky)/cholesky | solution.py:19
  492.7 0.7 select_reduce_fusion.1
  494.0 9.8 %custom-call.68 = f32[1,128,128]{1,2,0:T(8,128)S(1)} custom-call(f32[1,128,128]{2,1,0:T(8,128)S(1)} %get-tuple-element.26), custom_call_target="InvertDiagBlocksLowerTriangular" | custom-call | tf_op jit(solution)/shard_map/jit(cholesky)/cholesky | solution.py:19
  503.8 0.8 convolution_dynamic-update-slice_fusion.5
  504.6 1.8 convolution_subtract_fusion.10
  506.4 11.7 %cholesky.564 = f32[128,128]{1,0:T(8,128)S(1)} custom-call(f32[128,128]{1,0:T(8,128)S(1)} %convolution_subtract_fusion.10), custom_call_target="Cholesky" | custom-call | tf_op jit(solution)/shard_map/jit(cholesky)/cholesky | solution.py:19
  518.1 0.6 select_reduce_fusion
  519.4 0.7 compare_reduce_fusion.6
  525.0 4.8 select_select_fusion
  529.8 23.1 %while.1 = (s32[]{:T(128)}, f32[1024,1024]{1,0:T(8,128)}, s32[8,2]{0,1:T(2,128)S(1)}, f32[8,128,128]{2,1,0:T(8,128)S(1)}, s32[]{:T(128)}) while((s32[]{:T(128)}, f32[1024,1024]{1,0:T(8,128)}, s32[8,2]{0,1:T(2,128)S(1)}, f32[8,128,128]{2,1,0:T(8,128)S(1)}, s32[]{:T(128)}) %tuple.38), condition=%wide.while_cond, body=%wide.while_body.sunk | while | flops 2 | bytes 131181 | solution.py:25
  530.4 2.3 bitcast_dynamic-update-slice_fusion.2
  533.3 2.3 bitcast_dynamic-update-slice_fusion.2
  536.2 2.3 bitcast_dynamic-update-slice_fusion.2
  539.1 2.3 bitcast_dynamic-update-slice_fusion.2
  542.0 2.3 bitcast_dynamic-update-slice_fusion.2
  544.9 2.3 bitcast_dynamic-update-slice_fusion.2
  547.8 2.3 bitcast_dynamic-update-slice_fusion.2
  550.7 2.2 bitcast_dynamic-update-slice_fusion.2
  552.9 78.8 %custom-call.69 = f32[8,128,128]{1,2,0:T(8,128)S(1)} custom-call(f32[8,128,128]{2,1,0:T(8,128)S(1)} %get-tuple-element.12), custom_call_target="InvertDiagBlocksLowerTriangular" | custom-call | tf_op jit(solution)/shard_map/triangular_solve | solution.py:25
  632.0 1.1 convolution_subtract_fusion.9
  633.4 1.3 convolution_subtract_fusion.8
  635.0 1.4 convolution_subtract_fusion.7
  636.7 1.5 convolution_subtract_fusion.12
  638.6 1.7 convolution_subtract_fusion.11
  640.6 1.8 convolution_subtract_fusion.13
  642.8 1.9 convolution_subtract_fusion.6
  645.1 14.7 %fusion.63 = f32[64,4096]{1,0:T(8,128)} fusion(f32[1024,64]{0,1:T(8,128)S(1)} %constant_dynamic-update-slice_fusion.18, f32[1024,4096]{1,0:T(8,128)} %all-gather.5.cloned.1.call-done), kind=kOutput, calls=%fused_computation.159 | convolution fusion | flops 3221225472 | bytes 18087936 | tf_op jit(solution)/shard_map/dot_general | solution.py:29
  (73 shorter events, 12.6 us)
Async XLA Ops:
  6.5 122.1 %all-gather.5.cloned.1.call-start = ((), (), s32[]{:S(2)}) async-start(), calls=%async_computation | async-start | bytes 17825792 | tf_op jit(solution)/shard_map/all_gather | solution.py:10
  7.3 236.5 %all-gather.9.cloned.1.call-start = ((), (), s32[]{:S(2)}) async-start(), calls=%async_computation.2 | async-start | bytes 4456448 | tf_op jit(solution)/shard_map/all_gather | solution.py:17
  149.1 160.8 %all-gather.7.cloned.1.call-start = ((), (), s32[]{:S(2)}) async-start(), calls=%async_computation.1 | async-start | bytes 4456448 | tf_op jit(solution)/shard_map/all_gather | solution.py:18
  320.1 1.9 copy-start
Sparse Core Ops, SparseCore 0:
  10.1 118.4 all-gather.4
  149.2 94.4 all-gather.8
  247.0 62.7 all-gather.6
